TPU v7x, 128 devices: a whole 4x4x4 slice. The times are simulated.
128 devices in a mesh: px: 8 (over x, y_lo), pc: 16 (over z, y_hi, core).
Axes of the slice: x: 4, y: 4 (y_hi: 2, y_lo: 2; y = y_hi * 2 + y_lo), z: 4, core: 2. Of those that a mesh axis runs over, the one named last changes fastest.
Arguments:
- field: bfloat16 [64, 512, 1, 1024], P('pc', None, None, 'px'), may hold values from -6 to 6
- cotangent: bfloat16 [64, 512, 1, 1024], P(None, ('px', 'pc')), may hold values from -6 to 6
- kernel_z: bfloat16 [64, 31], P('pc'), may hold values from -1 to 1
- kernel_x: bfloat16 [64, 31], P('pc'), may hold values from -1 to 1
- weight_in: bfloat16 [64, 128], replicated, may hold values from -0.75 to 0.75
- weight_out: bfloat16 [128, 64], replicated, may hold values from -0.5 to 0.5
Outputs:
- result: bfloat16 [64, 512, 1, 1024], P(None, ('px', 'pc'))
- grad_field: bfloat16 [64, 512, 1, 1024], P('pc', None, None, 'px')
- grad_kernel_z: float32 [64, 31], P('pc')
- grad_kernel_x: float32 [64, 31], P('pc')
- grad_weight_in: float32 [64, 128], replicated
- grad_weight_out: float32 [128, 64], replicated
All inputs are finite; a program needn't handle non-finite values.
Results may differ from a plain program's by a relative error of at most 0.0097.
Values may be sent and summed in bfloat16 or wider, within the bound.
A program may use at most 128 MiB of HBM per device.

v0:
```python
import functools
import math

import jax
import jax.numpy as jnp
from jax import lax
from jax.experimental import pallas as pl
from jax.experimental.pallas import tpu as pltpu
from jax.sharding import PartitionSpec as P

MESH = pl.DeviceIdType.MESH
BF = jnp.bfloat16
F32 = jnp.float32
GELU_A = math.sqrt(2.0 / math.pi)
GELU_B = 0.044715
CHUNKS = 2
SUB = 256


def mm(left, right):
    return lax.dot_general(left, right, (((1,), (0,)), ((), ())), preferred_element_type=F32)


def mm_nt(left, right):
    return lax.dot_general(left, right, (((1,), (1,)), ((), ())), preferred_element_type=F32)


def iota(shape, dim):
    return lax.broadcasted_iota(jnp.int32, shape, dim)


def ones_where(mask):
    return jnp.where(mask, 1.0, 0.0).astype(BF)


def band(row, rows):
    wide = jnp.broadcast_to(row, (rows, 256))
    return pltpu.roll(wide, 241, axis=1, stride=1, stride_axis=0)


def lag_row(product):
    rolled = pltpu.roll(product, 144, axis=1, stride=1, stride_axis=0)
    return jnp.sum(rolled, axis=0, keepdims=True)[:, :128]


def ext_rows(pieces):
    zero = jnp.zeros((64, 128), BF)
    columns = []
    for blk in range(4):
        after = pieces[2 * blk + 2] if blk < 3 else zero
        before = pieces[2 * blk - 1] if blk > 0 else zero
        columns.append(jnp.concatenate([pieces[2 * blk], pieces[2 * blk + 1], after, before], axis=0))
    return jnp.concatenate(columns, axis=1)


def ext_lanes(pieces):
    zero = jnp.zeros((64, 128), BF)
    low = iota((64, 128), 1) < 64
    rows = []
    for blk in range(8):
        after = pieces[blk + 1] if blk < 7 else zero
        before = pieces[blk - 1] if blk > 0 else zero
        edge = jnp.where(low, after, before)
        rows.append(jnp.concatenate([pieces[blk], edge], axis=1))
    return jnp.concatenate(rows, axis=0)


class Exchange:
    def __init__(self, axis, size, me, send, recv, base):
        self.axis, self.size, self.me = axis, size, me
        self.send, self.recv, self.base = send, recv, base
        self.copies = []

    def start(self, src_at, dst_at):
        for k in range(1, self.size):
            peer = lax.rem(self.me + k, self.size)
            copy = pltpu.make_async_remote_copy(
                src_ref=src_at(peer),
                dst_ref=dst_at(self.me),
                send_sem=self.send.at[self.base + k - 1],
                recv_sem=self.recv.at[self.base + k - 1],
                device_id={self.axis: peer},
                device_id_type=MESH,
            )
            copy.start()
            self.copies.append(copy)

    def wait(self):
        for copy in self.copies:
            copy.wait()


def kernel(
    npx, npc, scale,
    field, cot, taps, w_in, w_ot,
    res_out, gf_out, w_out, k_out,
    fe, bands, xs, xr, xe, mx, ss, sr, mixd, cotp, resp, bkp, bs, br, gbx, gs, gr,
    wacc, rs1, rs2, rs2s, wfin, kxp, kxr, kzp, kzr,
    send, recv,
):
    px = lax.axis_index("px")
    pc = lax.axis_index("pc")
    lanes = 1024 // CHUNKS

    barrier = pltpu.get_barrier_semaphore()
    for k in range(1, npx):
        pl.semaphore_signal(barrier, inc=1, device_id={"px": lax.rem(px + k, npx)}, device_id_type=MESH)
    for k in range(1, npc):
        pl.semaphore_signal(barrier, inc=1, device_id={"pc": lax.rem(pc + k, npc)}, device_id_type=MESH)

    base = [0]

    def px_exchange():
        made = Exchange("px", npx, px, send, recv, base[0])
        base[0] += npx - 1
        return made

    def pc_exchange():
        made = Exchange("pc", npc, pc, send, recv, base[0])
        base[0] += npc - 1
        return made

    first = [px_exchange() for _ in range(4)]
    for c in range(4):
        ext = ext_rows([field[c, 64 * q : 64 * q + 64, :] for q in range(8)])
        fe[c] = ext
        made = mm(band(taps[c : c + 1, :], 128).astype(BF), ext).astype(BF)
        for blk in range(4):
            for half in range(2):
                xs[2 * blk + half, c] = made[64 * half : 64 * half + 64, 128 * blk : 128 * blk + 128]
        if c == 0:
            pl.semaphore_wait(barrier, npx + npc - 2)
        first[c].start(lambda peer: xs.at[peer, c], lambda slot: xr.at[slot, c])
    xr[px] = xs[px]

    for c in range(4):
        bands[c] = band(taps[12 + c : 13 + c, :], 256)[:, :128].astype(BF)
        bands[4 + c] = band(taps[8 + c : 9 + c, :], 256)[:, :128].astype(BF)
    shape = (256, 256)
    row, col = iota(shape, 0), iota(shape, 1)
    to_dest = ones_where(col == ((row // 4) % 4) * 64 + (row // 16) * 4 + row % 4)
    from_dest = ones_where(row == ((col // 4) % 4) * 64 + (col // 16) * 4 + col % 4)
    to_cells = ones_where(col == (row % 64) * 4 + row // 64)
    from_cells = ones_where(row == (col % 64) * 4 + col // 64)
    eye = ones_where(iota((128, 128), 0) == iota((128, 128), 1))
    flip = ones_where(iota((128, 128), 0) + iota((128, 128), 1) == 127)
    for part in range(4):
        at = slice(256 * part, 256 * part + 256)
        cotp[:, at] = mm(to_cells, cot[:, at]).astype(BF)
    w_in_v = w_in[...]
    w_ot_v = w_ot[...]
    w_in_t = mm_nt(eye, w_in_v).astype(BF)
    w_o_v = mm_nt(eye, w_ot_v).astype(BF)
    wacc[...] = jnp.zeros_like(wacc)

    for c in range(4):
        first[c].wait()
        ext = ext_lanes([xr[b, c] for b in range(8)])
        xe[c] = ext
        made = mm(ext, bands[c]).astype(BF)
        for b in range(8):
            mx[64 * c : 64 * c + 64, 128 * b : 128 * b + 128] = made[64 * b : 64 * b + 64, :]

    second = [pc_exchange() for _ in range(CHUNKS)]
    for h in range(CHUNKS):
        made = mm(to_dest, mx[:, lanes * h : lanes * h + lanes]).astype(BF)
        ss[h] = made.reshape(npc, 16, lanes)
        second[h].start(lambda peer: ss.at[h, peer], lambda slot: sr.at[h, slot])
        sr[h, pc] = ss[h, pc]

    third = [pc_exchange() for _ in range(CHUNKS)]
    for h in range(CHUNKS):
        second[h].wait()
        mixd[...] = mm(to_cells, sr[h].reshape(256, lanes)).astype(BF)

        def cells(step, carry):
            zz = step // (lanes // SUB)
            part = lax.rem(step, lanes // SUB)
            rows = pl.ds(pl.multiple_of(zz * 64, 64), 64)
            here = pl.ds(pl.multiple_of(part * SUB, SUB), SUB)
            there = pl.ds(pl.multiple_of(lanes * h + part * SUB, SUB), SUB)
            mixed = mixd[rows, here].astype(F32)
            cot_b = cotp[rows, there]
            centre = jnp.mean(mixed, axis=0, keepdims=True)
            shifted = mixed - centre
            inv_std = lax.rsqrt(jnp.mean(shifted * shifted, axis=0, keepdims=True) + 1e-06)
            normed = shifted * inv_std
            low = normed.astype(BF)
            v = mm(w_in_t, low)
            grad_act = mm(w_o_v, cot_b)
            v2 = v * v
            u = v * (GELU_A + (GELU_A * GELU_B) * v2)
            gate = 0.5 + 0.5 * jnp.tanh(u)
            act = v * gate
            slope = 2.0 * GELU_A + (6.0 * GELU_A * GELU_B) * v2
            act_low = act.astype(BF)
            grad_hid = (grad_act * (gate + act * (1.0 - gate) * slope)).astype(BF)
            resp[rows, here] = (mixed + mm(w_ot_v, act_low)).astype(BF)
            grad_n = mm(w_in_v, grad_hid)
            average = jnp.mean(grad_n, axis=0, keepdims=True)
            project = jnp.mean(grad_n * normed, axis=0, keepdims=True)
            bkp[rows, here] = (
                cot_b.astype(F32) + inv_std * (grad_n - average - normed * project)
            ).astype(BF)
            wacc[0:64, :] += mm_nt(cot_b, act_low)
            wacc[64:128, :] += mm_nt(low, grad_hid)
            return carry

        lax.fori_loop(0, 4 * (lanes // SUB), cells, 0)
        bs[h] = mm(from_cells, bkp[...]).astype(BF).reshape(npc, 16, lanes)
        third[h].start(lambda peer: bs.at[h, peer], lambda slot: br.at[h, slot])
        br[h, pc] = bs[h, pc]
        res_out[:, lanes * h : lanes * h + lanes] = mm(from_cells, resp[...]).astype(BF)

    wide1 = pc_exchange()
    wide1.start(lambda peer: wacc.at[pl.ds(pl.multiple_of(peer * 8, 8), 8)], lambda slot: rs1.at[slot])
    rs1[pc] = wacc[pl.ds(pl.multiple_of(pc * 8, 8), 8), :]

    for h in range(CHUNKS):
        third[h].wait()
        gbx[:, lanes * h : lanes * h + lanes] = mm(from_dest, br[h].reshape(256, lanes)).astype(BF)

    wide1.wait()
    rs2s[...] = jnp.sum(rs1[...], axis=0)
    wide2 = px_exchange()
    wide2.start(lambda peer: rs2s, lambda slot: rs2.at[slot])
    rs2[px] = rs2s[...]

    fourth = [px_exchange() for _ in range(4)]
    for c in range(4):
        pieces = [gbx[64 * c : 64 * c + 64, 128 * b : 128 * b + 128] for b in range(8)]
        made = mm(ext_lanes(pieces), bands[4 + c]).astype(BF)
        for b in range(8):
            gs[b, c] = made[64 * b : 64 * b + 64, :]
        fourth[c].start(lambda peer: gs.at[peer, c], lambda slot: gr.at[slot, c])
    gr[px] = gs[px]

    kxp[...] = jnp.zeros_like(kxp)
    for c in range(4):
        stacked = jnp.concatenate(
            [gbx[64 * c : 64 * c + 64, 128 * b : 128 * b + 128] for b in range(8)], axis=0
        )
        turned = mm_nt(flip, stacked).astype(BF)
        kxp[c : c + 1, :] = lag_row(mm(turned, xe[c]))
    kx_ex = px_exchange()
    kx_ex.start(lambda peer: kxp, lambda slot: kxr.at[slot])
    kxr[px] = kxp[...]

    wide2.wait()
    mine = pl.ds(pl.multiple_of(pc * 8, 8), 8)
    wfin[mine, :] = jnp.sum(rs2[...], axis=0) * scale
    wide3 = pc_exchange()
    wide3.start(lambda peer: wfin.at[mine], lambda slot: wfin.at[pl.ds(pl.multiple_of(slot * 8, 8), 8)])

    kzp[...] = jnp.zeros_like(kzp)
    exts = []
    for c in range(4):
        fourth[c].wait()
        ext = ext_rows([gr[q, c] for q in range(8)])
        exts.append(ext)
        turned = mm(flip, ext[:128, :]).astype(BF)
        kzp[c : c + 1, :] = lag_row(mm_nt(turned, fe[c]))
    kz_ex = px_exchange()
    kz_ex.start(lambda peer: kzp, lambda slot: kzr.at[slot])
    kzr[px] = kzp[...]
    for c in range(4):
        made = mm(band(taps[4 + c : 5 + c, :], 128).astype(BF), exts[c]).astype(BF)
        for blk in range(4):
            gf_out[c, 128 * blk : 128 * blk + 128, :] = made[:, 128 * blk : 128 * blk + 128]
    wide3.wait()
    w_out[...] = wfin[...]
    kx_ex.wait()
    k_out[0:8, :] = jnp.sum(kxr[...], axis=0) * scale
    kz_ex.wait()
    k_out[8:16, :] = jnp.sum(kzr[...], axis=0) * scale


def local(npx, npc, field, cotangent, kernel_z, kernel_x, weight_in, weight_out):
    lanes = 1024 // CHUNKS
    pad = [(0, 0), (0, 256 - 31)]
    taps = jnp.concatenate(
        [jnp.pad(k, pad) for k in (kernel_z, kernel_z[:, ::-1], kernel_x, kernel_x[:, ::-1])], axis=0
    ).astype(F32)
    copies = (4 + 4 + 1 + 1 + 1) * (npx - 1) + (2 * CHUNKS + 2) * (npc - 1)
    vmem = pl.BlockSpec(memory_space=pltpu.VMEM)
    scale = 1.0 / math.sqrt(512 * 1024)
    res, gf, w, k = pl.pallas_call(
        functools.partial(kernel, npx, npc, scale),
        out_shape=(
            jax.ShapeDtypeStruct((256, 1024), BF),
            jax.ShapeDtypeStruct((4, 512, 128), BF),
            jax.ShapeDtypeStruct((128, 128), F32),
            jax.ShapeDtypeStruct((16, 128), F32),
        ),
        in_specs=[vmem] * 5,
        out_specs=(vmem,) * 4,
        scratch_shapes=[
            pltpu.VMEM((4, 256, 512), BF),
            pltpu.VMEM((8, 256, 128), BF),
            pltpu.VMEM((8, 4, 64, 128), BF),
            pltpu.VMEM((8, 4, 64, 128), BF),
            pltpu.VMEM((4, 512, 256), BF),
            pltpu.VMEM((256, 1024), BF),
            pltpu.VMEM((CHUNKS, 16, 16, lanes), BF),
            pltpu.VMEM((CHUNKS, 16, 16, lanes), BF),
            pltpu.VMEM((256, lanes), BF),
            pltpu.VMEM((256, 1024), BF),
            pltpu.VMEM((256, lanes), BF),
            pltpu.VMEM((256, lanes), BF),
            pltpu.VMEM((CHUNKS, 16, 16, lanes), BF),
            pltpu.VMEM((CHUNKS, 16, 16, lanes), BF),
            pltpu.VMEM((256, 1024), BF),
            pltpu.VMEM((8, 4, 64, 128), BF),
            pltpu.VMEM((8, 4, 64, 128), BF),
            pltpu.VMEM((128, 128), F32),
            pltpu.VMEM((16, 8, 128), F32),
            pltpu.VMEM((8, 8, 128), F32),
            pltpu.VMEM((8, 128), F32),
            pltpu.VMEM((128, 128), F32),
            pltpu.VMEM((8, 128), F32),
            pltpu.VMEM((8, 8, 128), F32),
            pltpu.VMEM((8, 128), F32),
            pltpu.VMEM((8, 8, 128), F32),
            pltpu.SemaphoreType.DMA((copies,)),
            pltpu.SemaphoreType.DMA((copies,)),
        ],
        compiler_params=pltpu.CompilerParams(
            collective_id=0, has_side_effects=True, vmem_limit_bytes=56 * 1024 * 1024
        ),
    )(
        field.reshape(4, 512, 128),
        cotangent.reshape(256, 1024),
        taps,
        weight_in,
        weight_out.T,
    )
    return (
        res.reshape(64, 4, 1, 1024),
        gf.reshape(4, 512, 1, 128),
        k[8:12, :31],
        k[0:4, :31],
        w[64:128],
        w[0:64].T,
    )


def solution(mesh):
    placed = (
        P("pc", None, None, "px"),
        P(None, ("px", "pc"), None, None),
        P("pc", None),
        P("pc", None),
        P(),
        P(),
    )
    return jax.shard_map(
        functools.partial(local, mesh.shape["px"], mesh.shape["pc"]),
        mesh=mesh,
        in_specs=placed,
        out_specs=(
            P(None, ("px", "pc"), None, None),
            P("pc", None, None, "px"),
            P("pc", None),
            P("pc", None),
            P(),
            P(),
        ),
        check_vma=False,
    )
```

profile of v0, /device:TPU:1, one launch (start us, length us, event | category | flops | bytes accessed | tf_op | source)
XLA Modules:
  0.0 66.5 jit_solution(4923980225220069181)
XLA Ops:
  0.6 0.0 copy-start.3
  0.6 0.7 %copy-done.3 = bf16[4,31]{1,0:T(4,128)(2,1)S(1)} copy-done((bf16[4,31]{1,0:T(4,128)(2,1)S(1)}, bf16[4,31]{1,0:T(4,128)(2,1)}, u32[]{:S(2)}) %copy-start.3) | copy-done | bytes 272
  1.3 0.0 copy-start.2
  1.3 0.1 rev.6
  1.4 0.6 copy-done.2
  2.0 0.1 rev.7
  2.1 0.6 fusion.8.taps
  2.7 2.0 %reshape.25.cot = bf16[256,1024]{1,0:T(8,128)(2,1)} reshape(bf16[64,4,1,1024]{3,1,2,0:T(4,128)(2,1)} %param.7) | data formatting | bytes 1048576 | tf_op jit(solution)/shard_map/reshape | solution.py:332
  4.7 57.7 %shard_map.109 = (bf16[256,1024]{1,0:T(8,128)(2,1)}, bf16[4,512,128]{2,1,0:T(8,128)(2,1)}, f32[128,128]{1,0:T(8,128)}, f32[16,128]{1,0:T(8,128)}) custom-call(bf16[4,512,128]{2,1,0:T(8,128)(2,1)} %bitcast.10, bf16[256,1024]{1,0:T(8,128)(2,1)} %reshape.25.cot, f32[16,256]{1,0:T(8,128)} %fusion.8.taps, bf16[64,128]{1,0:T(8,128)(2,1)} %w_in.1, ...), custom_call_target="tpu_custom_call" | custom-call | tf_op jit(solution)/shard_map/pallas_call | solution.py:287
  62.3 0.0 copy-start.4
  62.4 0.0 copy-start.1
  62.4 0.0 copy-start
  62.4 2.1 %reshape.26 = bf16[64,4,1,1024]{3,1,0,2:T(4,128)(2,1)} reshape(bf16[256,1024]{1,0:T(8,128)(2,1)} %get-tuple-element.10) | data formatting | bytes 1048576 | tf_op jit(solution)/shard_map/reshape | solution.py:338
  64.5 0.0 copy-done.4
  64.5 0.6 fusion.10
  65.1 0.0 copy-done.1
  65.1 0.6 slice_bitcast_fusion
  65.7 0.0 copy-done
  65.7 0.8 %copy.15 = bf16[4,512,1,128]{3,1,2,0:T(8,128)(2,1)} copy(bf16[4,512,1,128]{3,1,2,0:T(8,128)(2,1)S(1)} %bitcast.12) | data formatting | bytes 1048576
Async XLA Ops:
  0.6 0.7 %copy-start.3 = (bf16[4,31]{1,0:T(4,128)(2,1)S(1)}, bf16[4,31]{1,0:T(4,128)(2,1)}, u32[]{:S(2)}) copy-start(bf16[4,31]{1,0:T(4,128)(2,1)} %param.8) | copy-start | bytes 748
  1.3 0.7 %copy-start.2 = (bf16[4,31]{1,0:T(4,128)(2,1)S(1)}, bf16[4,31]{1,0:T(4,128)(2,1)}, u32[]{:S(2)}) copy-start(bf16[4,31]{1,0:T(4,128)(2,1)} %param.9) | copy-start | bytes 748
  62.3 2.1 %copy-start.4 = (f32[16,128]{1,0:T(8,128)S(1)}, f32[16,128]{1,0:T(8,128)}, u32[]{:S(2)}) copy-start(f32[16,128]{1,0:T(8,128)} %get-tuple-element.12) | copy-start | bytes 24580
  62.4 2.7 %copy-start.1 = (f32[128,128]{1,0:T(8,128)S(1)}, f32[128,128]{1,0:T(8,128)}, u32[]{:S(2)}) copy-start(f32[128,128]{1,0:T(8,128)} %get-tuple-element.13) | copy-start | bytes 196612
  62.4 3.3 %copy-start = (bf16[4,512,128]{2,1,0:T(8,128)(2,1)S(1)}, bf16[4,512,128]{2,1,0:T(8,128)(2,1)}, u32[]{:S(2)}) copy-start(bf16[4,512,128]{2,1,0:T(8,128)(2,1)} %get-tuple-element.11) | copy-start | bytes 1572868
where the time goes:
time: 67.2 us; the launch traced here: 66.5 us
  Pallas kernels  57.7 us (86%)
  local copies, waits for them, and re-layouts  7.51 us (11%)
  between operations  0.68 us (1%)
    pallas_call x1, Pallas kernels, local(): pl.pallas_call(functools.partial(kernel, npx, npc, scale), out_shape=(jax...  57.7 us
    reshape x1, local copies, waits for them, and re-layouts, local(): res.reshape(64, 4, 1, 1024)  2.09 us
    unnamed x11, local copies, waits for them, and re-layouts  2.06 us
    reshape x1, local copies, waits for them, and re-layouts, local(): cotangent.reshape(256, 1024)  1.95 us

commit v1 on v0

v1 whole, which is shorter than its diff:
```python
import functools
import math

import jax
import jax.numpy as jnp
from jax import lax
from jax.experimental import pallas as pl
from jax.experimental.pallas import tpu as pltpu
from jax.sharding import PartitionSpec as P

MESH = pl.DeviceIdType.MESH
BF = jnp.bfloat16
F32 = jnp.float32
GELU_A = math.sqrt(2.0 / math.pi)
GELU_B = 0.044715


def mm(left, right):
    return lax.dot_general(left, right, (((1,), (0,)), ((), ())), preferred_element_type=F32)


def mm_nt(left, right):
    return lax.dot_general(left, right, (((1,), (1,)), ((), ())), preferred_element_type=F32)


def iota(shape, dim):
    return lax.broadcasted_iota(jnp.int32, shape, dim)


def ones_where(mask):
    return jnp.where(mask, 1.0, 0.0).astype(BF)


def band(row, rows):
    wide = jnp.broadcast_to(row, (rows, 256))
    return pltpu.roll(wide, 241, axis=1, stride=1, stride_axis=0)


def lag_row(product):
    rolled = pltpu.roll(product, 144, axis=1, stride=1, stride_axis=0)
    return jnp.sum(rolled, axis=0, keepdims=True)[:, :128]


def ext_rows(pieces):
    zero = jnp.zeros((64, 128), BF)
    columns = []
    for blk in range(4):
        after = pieces[2 * blk + 2] if blk < 3 else zero
        before = pieces[2 * blk - 1] if blk > 0 else zero
        columns.append(jnp.concatenate([pieces[2 * blk], pieces[2 * blk + 1], after, before], axis=0))
    return jnp.concatenate(columns, axis=1)


def tile(sheet, c, i):
    return sheet[64 * c : 64 * c + 64, 128 * i : 128 * i + 128]


def stack_lanes(sheet, edges, c):
    return jnp.concatenate(
        [jnp.concatenate([tile(sheet, c, i), tile(edges, c, i)], axis=1) for i in range(8)], axis=0
    )


class Exchange:
    def __init__(self, axis, size, me, send, recv, base):
        self.axis, self.size, self.me = axis, size, me
        self.send, self.recv, self.base = send, recv, base
        self.copies = []

    def start(self, src_at, dst_at):
        for k in range(1, self.size):
            peer = lax.rem(self.me + k, self.size)
            copy = pltpu.make_async_remote_copy(
                src_ref=src_at(peer),
                dst_ref=dst_at(self.me),
                send_sem=self.send.at[self.base + k - 1],
                recv_sem=self.recv.at[self.base + k - 1],
                device_id={self.axis: peer},
                device_id_type=MESH,
            )
            copy.start()
            self.copies.append(copy)

    def wait(self):
        for copy in self.copies:
            copy.wait()


def kernel(
    npx, npc, scale,
    field, cot, taps, w_in, w_ot,
    res_out, gf_out, w_out, k_out,
    fe, bands, az, hs, hr, xe, mx, ss, sr, mixd, cotp, resp, bkp, bs, br, gbx, hs2, hr2,
    wacc, rs1, rs2, rs2s, wfin, kp, kr,
    send, recv, all_send, all_recv, halo_send, halo_recv,
):
    px = lax.axis_index("px")
    pc = lax.axis_index("pc")

    barrier = pltpu.get_barrier_semaphore()

    def greet(k, carry):
        peer = lax.rem(px * npc + pc + k, npx * npc)
        pl.semaphore_signal(
            barrier, inc=1, device_id=(peer // npc, lax.rem(peer, npc)), device_id_type=MESH
        )
        return carry

    lax.fori_loop(1, npx * npc, greet, 0)

    base = [0]

    def px_exchange():
        made = Exchange("px", npx, px, send, recv, base[0])
        base[0] += npx - 1
        return made

    def pc_exchange():
        made = Exchange("pc", npc, pc, send, recv, base[0])
        base[0] += npc - 1
        return made

    def spread(which, step, direction, src, dst):
        peer_px = lax.rem(px + npx + direction * step, npx)
        slot = which * npx + step

        def one(k, carry):
            peer_pc = lax.rem(pc + k, npc)
            pltpu.make_async_remote_copy(
                src_ref=src.at[peer_px, peer_pc],
                dst_ref=dst.at[px, pc],
                send_sem=all_send.at[slot],
                recv_sem=all_recv.at[slot],
                device_id=(peer_px, peer_pc),
                device_id_type=MESH,
            ).start()
            return carry

        if step == 0:
            pltpu.make_async_copy(src.at[px, pc], dst.at[px, pc], all_recv.at[slot]).start()
        lax.fori_loop(1 if step == 0 else 0, npc, one, 0)

    def spread_arrived(which, step, direction, dst):
        from_px = lax.rem(px + npx - direction * step, npx)
        slot = which * npx + step
        whole = dst.at[from_px]
        pltpu.make_async_copy(whole, whole, all_recv.at[slot]).wait()
        return from_px

    def spread_left(which, step, src):
        slot = which * npx + step
        whole = src.at[0] if step else src.at[0, pl.ds(0, npc - 1)]
        pltpu.make_async_copy(whole, whole, all_send.at[slot]).wait()

    def halo_start(which, sheet, pick, out, into):
        packed = mm(sheet[...], pick).astype(BF)
        copies = []
        for side in range(2):
            out[side] = packed[:, 128 * side : 128 * side + 128]
            copy = pltpu.make_async_remote_copy(
                src_ref=out.at[side],
                dst_ref=into.at[side],
                send_sem=halo_send.at[2 * which + side],
                recv_sem=halo_recv.at[2 * which + side],
                device_id={"px": lax.rem(px + (npx - 1 if side == 0 else 1), npx)},
                device_id_type=MESH,
            )
            copy.start()
            copies.append(copy)
        return copies

    def halo_end(copies, pick, into):
        for copy in copies:
            copy.wait()
        keep_after = jnp.where(px < npx - 1, 1.0, 0.0).astype(F32)
        keep_before = jnp.where(px > 0, 1.0, 0.0).astype(F32)
        after = (into[0].astype(F32) * keep_after).astype(BF)
        before = (into[1].astype(F32) * keep_before).astype(BF)
        return mm_nt(jnp.concatenate([after, before], axis=1), pick).astype(BF)

    for c in range(4):
        ext = ext_rows([field[c, 64 * q : 64 * q + 64, :] for q in range(8)])
        fe[c] = ext
        made = mm(band(taps[c : c + 1, :], 128).astype(BF), ext).astype(BF)
        for blk in range(4):
            for half in range(2):
                i = 2 * blk + half
                az[64 * c : 64 * c + 64, 128 * i : 128 * i + 128] = made[
                    64 * half : 64 * half + 64, 128 * blk : 128 * blk + 128
                ]
    row, col = iota((1024, 256), 0), iota((1024, 256), 1)
    pick = ones_where(
        (row // 128 == (col % 128) // 16) & (row % 128 == col % 16 + jnp.where(col < 128, 0, 112))
    )
    pl.semaphore_wait(barrier, npx * npc - 1)
    halo = halo_start(0, az, pick, hs, hr)

    for c in range(4):
        bands[c] = band(taps[12 + c : 13 + c, :], 256)[:, :128].astype(BF)
        bands[4 + c] = band(taps[8 + c : 9 + c, :], 256)[:, :128].astype(BF)
    shape = (256, 256)
    row, col = iota(shape, 0), iota(shape, 1)
    to_dest = ones_where(col == ((row // 4) % 4) * 64 + (row // 16) * 4 + row % 4)
    from_dest = ones_where(row == ((col // 4) % 4) * 64 + (col // 16) * 4 + col % 4)
    to_cells = ones_where(col == (row % 64) * 4 + row // 64)
    from_cells = ones_where(row == (col % 64) * 4 + col // 64)
    eye = ones_where(iota((128, 128), 0) == iota((128, 128), 1))
    flip = ones_where(iota((128, 128), 0) + iota((128, 128), 1) == 127)
    for part in range(4):
        made = mm(to_cells, cot[:, 256 * part : 256 * part + 256]).astype(BF)
        cotp[2 * part] = made[:, :128]
        cotp[2 * part + 1] = made[:, 128:]
    w_in_v = w_in[...]
    w_ot_v = w_ot[...]
    w_in_t = mm_nt(eye, w_in_v).astype(BF)
    w_o_v = mm_nt(eye, w_ot_v).astype(BF)
    wacc[...] = jnp.zeros_like(wacc)

    edges = halo_end(halo, pick, hr)
    for c in range(4):
        ext = stack_lanes(az, edges, c)
        xe[c] = ext
        made = mm(ext, bands[c]).astype(BF)
        for i in range(8):
            mx[64 * c : 64 * c + 64, 128 * i : 128 * i + 128] = made[64 * i : 64 * i + 64, :]

    for part in range(4):
        made = mm(to_dest, mx[:, 256 * part : 256 * part + 256]).astype(BF)
        ss[2 * part] = made[:, :128].reshape(npc, 16, 128)
        ss[2 * part + 1] = made[:, 128:].reshape(npc, 16, 128)
    for step in range(npx):
        spread(0, step, -1, ss, sr)

    for pair in range(4):
        i0 = spread_arrived(0, 2 * pair, -1, sr)
        i1 = spread_arrived(0, 2 * pair + 1, -1, sr)
        both = jnp.concatenate([sr[i0].reshape(256, 128), sr[i1].reshape(256, 128)], axis=1)
        mixd[...] = mm(to_cells, both).astype(BF)

        def cells(zz, carry):
            rows = pl.ds(pl.multiple_of(zz * 64, 64), 64)
            mixed = mixd[rows, :].astype(F32)
            cot_b = jnp.concatenate([cotp[i0, rows, :], cotp[i1, rows, :]], axis=1)
            centre = jnp.mean(mixed, axis=0, keepdims=True)
            shifted = mixed - centre
            inv_std = lax.rsqrt(jnp.mean(shifted * shifted, axis=0, keepdims=True) + 1e-06)
            normed = shifted * inv_std
            low = normed.astype(BF)
            v = mm(w_in_t, low)
            grad_act = mm(w_o_v, cot_b)
            v2 = v * v
            u = v * (GELU_A + (GELU_A * GELU_B) * v2)
            gate = 0.5 + 0.5 * jnp.tanh(u)
            act = v * gate
            slope = 2.0 * GELU_A + (6.0 * GELU_A * GELU_B) * v2
            act_low = act.astype(BF)
            grad_hid = (grad_act * (gate + act * (1.0 - gate) * slope)).astype(BF)
            resp[rows, :] = (mixed + mm(w_ot_v, act_low)).astype(BF)
            grad_n = mm(w_in_v, grad_hid)
            average = jnp.mean(grad_n, axis=0, keepdims=True)
            project = jnp.mean(grad_n * normed, axis=0, keepdims=True)
            bkp[rows, :] = (
                cot_b.astype(F32) + inv_std * (grad_n - average - normed * project)
            ).astype(BF)
            wacc[0:64, :] += mm_nt(cot_b, act_low)
            wacc[64:128, :] += mm_nt(low, grad_hid)
            return carry

        lax.fori_loop(0, 4, cells, 0)
        made = mm(from_cells, bkp[...]).astype(BF)
        bs[i0] = made[:, :128].reshape(npc, 16, 128)
        bs[i1] = made[:, 128:].reshape(npc, 16, 128)
        spread(1, 2 * pair, 1, bs, br)
        spread(1, 2 * pair + 1, 1, bs, br)
        made = mm(from_cells, resp[...]).astype(BF)
        res_out[:, pl.ds(pl.multiple_of(i0 * 128, 128), 128)] = made[:, :128]
        res_out[:, pl.ds(pl.multiple_of(i1 * 128, 128), 128)] = made[:, 128:]

    wide1 = pc_exchange()
    wide1.start(lambda peer: wacc.at[pl.ds(pl.multiple_of(peer * 8, 8), 8)], lambda slot: rs1.at[slot])
    rs1[pc] = wacc[pl.ds(pl.multiple_of(pc * 8, 8), 8), :]

    for pair in range(4):
        i0 = spread_arrived(1, 2 * pair, 1, br)
        i1 = spread_arrived(1, 2 * pair + 1, 1, br)
        both = jnp.concatenate([br[i0].reshape(256, 128), br[i1].reshape(256, 128)], axis=1)
        made = mm(from_dest, both).astype(BF)
        gbx[:, pl.ds(pl.multiple_of(i0 * 128, 128), 128)] = made[:, :128]
        gbx[:, pl.ds(pl.multiple_of(i1 * 128, 128), 128)] = made[:, 128:]
    halo = halo_start(1, gbx, pick, hs2, hr2)

    wide1.wait()
    rs2s[...] = jnp.sum(rs1[...], axis=0)
    wide2 = px_exchange()
    wide2.start(lambda peer: rs2s, lambda slot: rs2.at[slot])
    rs2[px] = rs2s[...]

    kp[...] = jnp.zeros_like(kp)
    for c in range(4):
        stacked = jnp.concatenate([tile(gbx, c, i) for i in range(8)], axis=0)
        turned = mm_nt(flip, stacked).astype(BF)
        kp[c : c + 1, :] = lag_row(mm(turned, xe[c]))

    edges = halo_end(halo, pick, hr2)
    exts = []
    for c in range(4):
        made = mm(stack_lanes(gbx, edges, c), bands[4 + c]).astype(BF)
        ext = ext_rows([made[64 * q : 64 * q + 64, :] for q in range(8)])
        exts.append(ext)
        turned = mm(flip, ext[:128, :]).astype(BF)
        kp[4 + c : 5 + c, :] = lag_row(mm_nt(turned, fe[c]))
    k_ex = px_exchange()
    k_ex.start(lambda peer: kp, lambda slot: kr.at[slot])
    kr[px] = kp[...]

    wide2.wait()
    mine = pl.ds(pl.multiple_of(pc * 8, 8), 8)
    wfin[mine, :] = jnp.sum(rs2[...], axis=0) * scale
    wide3 = pc_exchange()
    wide3.start(lambda peer: wfin.at[mine], lambda slot: wfin.at[pl.ds(pl.multiple_of(slot * 8, 8), 8)])

    for c in range(4):
        made = mm(band(taps[4 + c : 5 + c, :], 128).astype(BF), exts[c]).astype(BF)
        for blk in range(4):
            gf_out[c, 128 * blk : 128 * blk + 128, :] = made[:, 128 * blk : 128 * blk + 128]
    for step in range(npx):
        spread_left(0, step, ss)
        spread_left(1, step, bs)
    k_ex.wait()
    k_out[...] = jnp.sum(kr[...], axis=0) * scale
    wide3.wait()
    w_out[...] = wfin[...]


def local(npx, npc, field, cotangent, kernel_z, kernel_x, weight_in, weight_out):
    pad = [(0, 0), (0, 256 - 31)]
    taps = jnp.concatenate(
        [jnp.pad(k, pad) for k in (kernel_z, kernel_z[:, ::-1], kernel_x, kernel_x[:, ::-1])], axis=0
    ).astype(F32)
    copies = 2 * (npx - 1) + 2 * (npc - 1)
    vmem = pl.BlockSpec(memory_space=pltpu.VMEM)
    scale = 1.0 / math.sqrt(512 * 1024)
    res, gf, w, k = pl.pallas_call(
        functools.partial(kernel, npx, npc, scale),
        out_shape=(
            jax.ShapeDtypeStruct((256, 1024), BF),
            jax.ShapeDtypeStruct((4, 512, 128), BF),
            jax.ShapeDtypeStruct((128, 128), F32),
            jax.ShapeDtypeStruct((8, 128), F32),
        ),
        in_specs=[vmem] * 5,
        out_specs=(vmem,) * 4,
        scratch_shapes=[
            pltpu.VMEM((4, 256, 512), BF),
            pltpu.VMEM((8, 256, 128), BF),
            pltpu.VMEM((256, 1024), BF),
            pltpu.VMEM((2, 256, 128), BF),
            pltpu.VMEM((2, 256, 128), BF),
            pltpu.VMEM((4, 512, 256), BF),
            pltpu.VMEM((256, 1024), BF),
            pltpu.VMEM((8, 16, 16, 128), BF),
            pltpu.VMEM((8, 16, 16, 128), BF),
            pltpu.VMEM((256, 256), BF),
            pltpu.VMEM((8, 256, 128), BF),
            pltpu.VMEM((256, 256), BF),
            pltpu.VMEM((256, 256), BF),
            pltpu.VMEM((8, 16, 16, 128), BF),
            pltpu.VMEM((8, 16, 16, 128), BF),
            pltpu.VMEM((256, 1024), BF),
            pltpu.VMEM((2, 256, 128), BF),
            pltpu.VMEM((2, 256, 128), BF),
            pltpu.VMEM((128, 128), F32),
            pltpu.VMEM((16, 8, 128), F32),
            pltpu.VMEM((8, 8, 128), F32),
            pltpu.VMEM((8, 128), F32),
            pltpu.VMEM((128, 128), F32),
            pltpu.VMEM((8, 128), F32),
            pltpu.VMEM((8, 8, 128), F32),
            pltpu.SemaphoreType.DMA((copies,)),
            pltpu.SemaphoreType.DMA((copies,)),
            pltpu.SemaphoreType.DMA((2 * npx,)),
            pltpu.SemaphoreType.DMA((2 * npx,)),
            pltpu.SemaphoreType.DMA((4,)),
            pltpu.SemaphoreType.DMA((4,)),
        ],
        compiler_params=pltpu.CompilerParams(
            collective_id=0, has_side_effects=True, vmem_limit_bytes=56 * 1024 * 1024
        ),
    )(
        field.reshape(4, 512, 128),
        cotangent.reshape(256, 1024),
        taps,
        weight_in,
        weight_out.T,
    )
    return (
        res.reshape(64, 4, 1, 1024),
        gf.reshape(4, 512, 1, 128),
        k[4:8, :31],
        k[0:4, :31],
        w[64:128],
        w[0:64].T,
    )


def solution(mesh):
    placed = (
        P("pc", None, None, "px"),
        P(None, ("px", "pc"), None, None),
        P("pc", None),
        P("pc", None),
        P(),
        P(),
    )
    return jax.shard_map(
        functools.partial(local, mesh.shape["px"], mesh.shape["pc"]),
        mesh=mesh,
        in_specs=placed,
        out_specs=(
            P(None, ("px", "pc"), None, None),
            P("pc", None, None, "px"),
            P("pc", None),
            P("pc", None),
            P(),
            P(),
        ),
        check_vma=False,
    )
```

time: 67.2 us -> 65.9 us (0.981)
  Pallas kernels: 57.7 us -> 56.9 us
    pallas_call x1, Pallas kernels: 57.7 us -> 56.9 us  [local(): pl.pallas_call(functools.partial(kernel, npx, npc, scale), out_shape=(jax...]
where the time goes in v1:
time: 65.9 us; the launch traced here: 65.7 us
  Pallas kernels  56.9 us (86%)
  local copies, waits for them, and re-layouts  7.51 us (11%)
  between operations  0.68 us (1%)
    pallas_call x1, Pallas kernels, local(): pl.pallas_call(functools.partial(kernel, npx, npc, scale), out_shape=(jax...  56.9 us
    reshape x1, local copies, waits for them, and re-layouts, local(): res.reshape(64, 4, 1, 1024)  2.09 us
    unnamed x11, local copies, waits for them, and re-layouts  2.06 us
    reshape x1, local copies, waits for them, and re-layouts, local(): cotangent.reshape(256, 1024)  1.95 us

profile of v1, /device:TPU:1, one launch (start us, length us, event | category | flops | bytes accessed | tf_op | source)
XLA Modules:
  0.0 65.7 jit_solution(2877001715274374211)
XLA Ops:
  0.6 0.0 copy-start.3
  0.6 0.7 %copy-done.3 = bf16[4,31]{1,0:T(4,128)(2,1)S(1)} copy-done((bf16[4,31]{1,0:T(4,128)(2,1)S(1)}, bf16[4,31]{1,0:T(4,128)(2,1)}, u32[]{:S(2)}) %copy-start.3) | copy-done | bytes 272
  1.3 0.0 copy-start.2
  1.3 0.1 rev.6
  1.4 0.6 copy-done.2
  2.0 0.1 rev.7
  2.1 0.6 fusion.8.taps
  2.7 2.0 %reshape.25.cot = bf16[256,1024]{1,0:T(8,128)(2,1)} reshape(bf16[64,4,1,1024]{3,1,2,0:T(4,128)(2,1)} %param.7) | data formatting | bytes 1048576 | tf_op jit(solution)/shard_map/reshape | solution.py:391
  4.7 56.9 %shard_map.109 = (bf16[256,1024]{1,0:T(8,128)(2,1)}, bf16[4,512,128]{2,1,0:T(8,128)(2,1)}, f32[128,128]{1,0:T(8,128)}, f32[8,128]{1,0:T(8,128)}) custom-call(bf16[4,512,128]{2,1,0:T(8,128)(2,1)} %bitcast.10, bf16[256,1024]{1,0:T(8,128)(2,1)} %reshape.25.cot, f32[16,256]{1,0:T(8,128)} %fusion.8.taps, bf16[64,128]{1,0:T(8,128)(2,1)} %w_in.1, ...), custom_call_target="tpu_custom_call" | custom-call | tf_op jit(solution)/shard_map/pallas_call | solution.py:343
  61.6 0.0 copy-start.4
  61.6 0.0 copy-start.1
  61.6 0.0 copy-start
  61.6 2.1 %reshape.26 = bf16[64,4,1,1024]{3,1,0,2:T(4,128)(2,1)} reshape(bf16[256,1024]{1,0:T(8,128)(2,1)} %get-tuple-element.10) | data formatting | bytes 1048576 | tf_op jit(solution)/shard_map/reshape | solution.py:397
  63.7 0.0 copy-done.4
  63.7 0.6 fusion.10
  64.3 0.0 copy-done.1
  64.3 0.6 slice_bitcast_fusion
  64.9 0.0 copy-done
  64.9 0.8 %copy.15 = bf16[4,512,1,128]{3,1,2,0:T(8,128)(2,1)} copy(bf16[4,512,1,128]{3,1,2,0:T(8,128)(2,1)S(1)} %bitcast.12) | data formatting | bytes 1048576
Async XLA Ops:
  0.6 0.7 %copy-start.3 = (bf16[4,31]{1,0:T(4,128)(2,1)S(1)}, bf16[4,31]{1,0:T(4,128)(2,1)}, u32[]{:S(2)}) copy-start(bf16[4,31]{1,0:T(4,128)(2,1)} %param.8) | copy-start | bytes 748
  1.3 0.7 %copy-start.2 = (bf16[4,31]{1,0:T(4,128)(2,1)S(1)}, bf16[4,31]{1,0:T(4,128)(2,1)}, u32[]{:S(2)}) copy-start(bf16[4,31]{1,0:T(4,128)(2,1)} %param.9) | copy-start | bytes 748
  61.6 2.1 %copy-start.4 = (f32[8,128]{1,0:T(8,128)S(1)}, f32[8,128]{1,0:T(8,128)}, u32[]{:S(2)}) copy-start(f32[8,128]{1,0:T(8,128)} %get-tuple-element.12) | copy-start | bytes 12292
  61.6 2.7 %copy-start.1 = (f32[128,128]{1,0:T(8,128)S(1)}, f32[128,128]{1,0:T(8,128)}, u32[]{:S(2)}) copy-start(f32[128,128]{1,0:T(8,128)} %get-tuple-element.13) | copy-start | bytes 196612
  61.6 3.3 %copy-start = (bf16[4,512,128]{2,1,0:T(8,128)(2,1)S(1)}, bf16[4,512,128]{2,1,0:T(8,128)(2,1)}, u32[]{:S(2)}) copy-start(bf16[4,512,128]{2,1,0:T(8,128)(2,1)} %get-tuple-element.11) | copy-start | bytes 1572868

commit v2 on v1

--- a/solution.py
+++ b/solution.py
@@ -88,9 +88,9 @@
 
 def kernel(
     npx, npc, scale,
-    field, cot, taps, w_in, w_ot,
-    res_out, gf_out, w_out, k_out,
-    fe, bands, az, hs, hr, xe, mx, ss, sr, mixd, cotp, resp, bkp, bs, br, gbx, hs2, hr2,
+    field, cot, kz, kx, w_in, w_ot,
+    res_out, gf_out, kz_out, kx_out, wi_out, wo_out,
+    taps, fs, kfe, bands, az, aze, hs, hr, xe, mx, ss, sr, mixd, cotp, resp, bkp, bs, br, gbx, hs2, hr2,
     wacc, rs1, rs2, rs2s, wfin, kp, kr,
     send, recv, all_send, all_recv, halo_send, halo_recv,
 ):
@@ -152,8 +152,7 @@
         whole = src.at[0] if step else src.at[0, pl.ds(0, npc - 1)]
         pltpu.make_async_copy(whole, whole, all_send.at[slot]).wait()
 
-    def halo_start(which, sheet, pick, out, into):
-        packed = mm(sheet[...], pick).astype(BF)
+    def halo_start(which, packed, out, into):
         copies = []
         for side in range(2):
             out[side] = packed[:, 128 * side : 128 * side + 128]
@@ -178,26 +177,40 @@
         before = (into[1].astype(F32) * keep_before).astype(BF)
         return mm_nt(jnp.concatenate([after, before], axis=1), pick).astype(BF)
 
-    for c in range(4):
-        ext = ext_rows([field[c, 64 * q : 64 * q + 64, :] for q in range(8)])
-        fe[c] = ext
-        made = mm(band(taps[c : c + 1, :], 128).astype(BF), ext).astype(BF)
-        for blk in range(4):
-            for half in range(2):
-                i = 2 * blk + half
-                az[64 * c : 64 * c + 64, 128 * i : 128 * i + 128] = made[
-                    64 * half : 64 * half + 64, 128 * blk : 128 * blk + 128
-                ]
+    taps[...] = jnp.zeros_like(taps)
+    taps[0:4, 0:31] = kz[...].astype(F32)
+    taps[8:12, 0:31] = kx[...].astype(F32)
+    back = ones_where(iota((128, 128), 0) + iota((128, 128), 1) == 30)
+    turned = mm(taps[:, 0:128].astype(BF), back)
+    taps[4:8, 0:128] = turned[0:4]
+    taps[12:16, 0:128] = turned[8:12]
+
     row, col = iota((1024, 256), 0), iota((1024, 256), 1)
     pick = ones_where(
         (row // 128 == (col % 128) // 16) & (row % 128 == col % 16 + jnp.where(col < 128, 0, 112))
     )
-    pl.semaphore_wait(barrier, npx * npc - 1)
-    halo = halo_start(0, az, pick, hs, hr)
+    for c in range(4):
+        for i in range(8):
+            fs[64 * c : 64 * c + 64, 128 * i : 128 * i + 128] = field[c, 64 * i : 64 * i + 64, :]
+    packed = mm(fs[...], pick).astype(BF)
+
+    def along_z(sheet, into):
+        for c in range(4):
+            ext = ext_rows([tile(sheet, c, i) for i in range(8)])
+            made = mm(band(taps[c : c + 1, :], 128).astype(BF), ext).astype(BF)
+            for i in range(8):
+                half = 64 * (i % 2)
+                into[64 * c : 64 * c + 64, 128 * i : 128 * i + 128] = made[
+                    half : half + 64, 128 * (i // 2) : 128 * (i // 2) + 128
+                ]
 
     for c in range(4):
         bands[c] = band(taps[12 + c : 13 + c, :], 256)[:, :128].astype(BF)
         bands[4 + c] = band(taps[8 + c : 9 + c, :], 256)[:, :128].astype(BF)
+    pl.semaphore_wait(barrier, npx * npc - 1)
+    halo = halo_start(0, packed, hs, hr)
+    along_z(fs, az)
+
     shape = (256, 256)
     row, col = iota(shape, 0), iota(shape, 1)
     to_dest = ones_where(col == ((row // 4) % 4) * 64 + (row // 16) * 4 + row % 4)
@@ -207,7 +220,8 @@
     eye = ones_where(iota((128, 128), 0) == iota((128, 128), 1))
     flip = ones_where(iota((128, 128), 0) + iota((128, 128), 1) == 127)
     for part in range(4):
-        made = mm(to_cells, cot[:, 256 * part : 256 * part + 256]).astype(BF)
+        flat = cot[:, :, 256 * part : 256 * part + 256].astype(F32).reshape(256, 256).astype(BF)
+        made = mm(to_cells, flat).astype(BF)
         cotp[2 * part] = made[:, :128]
         cotp[2 * part + 1] = made[:, 128:]
     w_in_v = w_in[...]
@@ -217,8 +231,9 @@
     wacc[...] = jnp.zeros_like(wacc)
 
     edges = halo_end(halo, pick, hr)
-    for c in range(4):
-        ext = stack_lanes(az, edges, c)
+    along_z(edges, aze)
+    for c in range(4):
+        ext = stack_lanes(az, aze, c)
         xe[c] = ext
         made = mm(ext, bands[c]).astype(BF)
         for i in range(8):
@@ -230,6 +245,10 @@
         ss[2 * part + 1] = made[:, 128:].reshape(npc, 16, 128)
     for step in range(npx):
         spread(0, step, -1, ss, sr)
+
+    for c in range(4):
+        made = mm(stack_lanes(fs, edges, c), bands[c]).astype(BF)
+        kfe[c] = ext_rows([made[64 * i : 64 * i + 64, :] for i in range(8)])
 
     for pair in range(4):
         i0 = spread_arrived(0, 2 * pair, -1, sr)
@@ -272,9 +291,9 @@
         bs[i1] = made[:, 128:].reshape(npc, 16, 128)
         spread(1, 2 * pair, 1, bs, br)
         spread(1, 2 * pair + 1, 1, bs, br)
-        made = mm(from_cells, resp[...]).astype(BF)
-        res_out[:, pl.ds(pl.multiple_of(i0 * 128, 128), 128)] = made[:, :128]
-        res_out[:, pl.ds(pl.multiple_of(i1 * 128, 128), 128)] = made[:, 128:]
+        made = mm(from_cells, resp[...]).reshape(64, 4, 256).astype(BF)
+        res_out[:, :, pl.ds(pl.multiple_of(i0 * 128, 128), 128)] = made[:, :, :128]
+        res_out[:, :, pl.ds(pl.multiple_of(i1 * 128, 128), 128)] = made[:, :, 128:]
 
     wide1 = pc_exchange()
     wide1.start(lambda peer: wacc.at[pl.ds(pl.multiple_of(peer * 8, 8), 8)], lambda slot: rs1.at[slot])
@@ -287,7 +306,7 @@
         made = mm(from_dest, both).astype(BF)
         gbx[:, pl.ds(pl.multiple_of(i0 * 128, 128), 128)] = made[:, :128]
         gbx[:, pl.ds(pl.multiple_of(i1 * 128, 128), 128)] = made[:, 128:]
-    halo = halo_start(1, gbx, pick, hs2, hr2)
+    halo = halo_start(1, mm(gbx[...], pick).astype(BF), hs2, hr2)
 
     wide1.wait()
     rs2s[...] = jnp.sum(rs1[...], axis=0)
@@ -295,20 +314,13 @@
     wide2.start(lambda peer: rs2s, lambda slot: rs2.at[slot])
     rs2[px] = rs2s[...]
 
-    kp[...] = jnp.zeros_like(kp)
-    for c in range(4):
-        stacked = jnp.concatenate([tile(gbx, c, i) for i in range(8)], axis=0)
-        turned = mm_nt(flip, stacked).astype(BF)
+    for c in range(4):
+        pieces = [tile(gbx, c, i) for i in range(8)]
+        turned = mm_nt(flip, jnp.concatenate(pieces, axis=0)).astype(BF)
         kp[c : c + 1, :] = lag_row(mm(turned, xe[c]))
-
-    edges = halo_end(halo, pick, hr2)
-    exts = []
-    for c in range(4):
-        made = mm(stack_lanes(gbx, edges, c), bands[4 + c]).astype(BF)
-        ext = ext_rows([made[64 * q : 64 * q + 64, :] for q in range(8)])
-        exts.append(ext)
-        turned = mm(flip, ext[:128, :]).astype(BF)
-        kp[4 + c : 5 + c, :] = lag_row(mm_nt(turned, fe[c]))
+        blocks = [jnp.concatenate(pieces[2 * b : 2 * b + 2], axis=0) for b in range(4)]
+        turned = mm(flip, jnp.concatenate(blocks, axis=1)).astype(BF)
+        kp[4 + c : 5 + c, :] = lag_row(mm_nt(turned, kfe[c]))
     k_ex = px_exchange()
     k_ex.start(lambda peer: kp, lambda slot: kr.at[slot])
     kr[px] = kp[...]
@@ -319,6 +331,11 @@
     wide3 = pc_exchange()
     wide3.start(lambda peer: wfin.at[mine], lambda slot: wfin.at[pl.ds(pl.multiple_of(slot * 8, 8), 8)])
 
+    edges = halo_end(halo, pick, hr2)
+    exts = []
+    for c in range(4):
+        made = mm(stack_lanes(gbx, edges, c), bands[4 + c]).astype(BF)
+        exts.append(ext_rows([made[64 * q : 64 * q + 64, :] for q in range(8)]))
     for c in range(4):
         made = mm(band(taps[4 + c : 5 + c, :], 128).astype(BF), exts[c]).astype(BF)
         for blk in range(4):
@@ -327,32 +344,42 @@
         spread_left(0, step, ss)
         spread_left(1, step, bs)
     k_ex.wait()
-    k_out[...] = jnp.sum(kr[...], axis=0) * scale
+    total = jnp.sum(kr[...], axis=0) * scale
+    kx_out[...] = total[0:4, :31]
+    kz_out[...] = total[4:8, :31]
     wide3.wait()
-    w_out[...] = wfin[...]
+    wo_out[...] = wfin[0:64, :]
+    wi_out[...] = wfin[64:128, :]
+
+
+def write_kernel(*refs):
+    half = len(refs) // 2
+    for source, target in zip(refs[:half], refs[half:]):
+        target[...] = source[...]
 
 
 def local(npx, npc, field, cotangent, kernel_z, kernel_x, weight_in, weight_out):
-    pad = [(0, 0), (0, 256 - 31)]
-    taps = jnp.concatenate(
-        [jnp.pad(k, pad) for k in (kernel_z, kernel_z[:, ::-1], kernel_x, kernel_x[:, ::-1])], axis=0
-    ).astype(F32)
     copies = 2 * (npx - 1) + 2 * (npc - 1)
     vmem = pl.BlockSpec(memory_space=pltpu.VMEM)
     scale = 1.0 / math.sqrt(512 * 1024)
-    res, gf, w, k = pl.pallas_call(
+    made = pl.pallas_call(
         functools.partial(kernel, npx, npc, scale),
         out_shape=(
-            jax.ShapeDtypeStruct((256, 1024), BF),
+            jax.ShapeDtypeStruct((64, 4, 1024), BF),
             jax.ShapeDtypeStruct((4, 512, 128), BF),
-            jax.ShapeDtypeStruct((128, 128), F32),
-            jax.ShapeDtypeStruct((8, 128), F32),
+            jax.ShapeDtypeStruct((4, 31), F32),
+            jax.ShapeDtypeStruct((4, 31), F32),
+            jax.ShapeDtypeStruct((64, 128), F32),
+            jax.ShapeDtypeStruct((64, 128), F32),
         ),
-        in_specs=[vmem] * 5,
-        out_specs=(vmem,) * 4,
+        in_specs=[vmem] * 6,
+        out_specs=(vmem,) * 6,
         scratch_shapes=[
+            pltpu.VMEM((16, 256), F32),
+            pltpu.VMEM((256, 1024), BF),
             pltpu.VMEM((4, 256, 512), BF),
             pltpu.VMEM((8, 256, 128), BF),
+            pltpu.VMEM((256, 1024), BF),
             pltpu.VMEM((256, 1024), BF),
             pltpu.VMEM((2, 256, 128), BF),
             pltpu.VMEM((2, 256, 128), BF),
@@ -388,18 +415,25 @@
         ),
     )(
         field.reshape(4, 512, 128),
-        cotangent.reshape(256, 1024),
-        taps,
+        cotangent.reshape(64, 4, 1024),
+        kernel_z,
+        kernel_x,
         weight_in,
         weight_out.T,
     )
+    res, gf, grad_kz, grad_kx, grad_in, grad_out = pl.pallas_call(
+        write_kernel,
+        out_shape=tuple(jax.ShapeDtypeStruct(m.shape, m.dtype) for m in made),
+        in_specs=[vmem] * 6,
+        out_specs=(vmem,) * 6,
+    )(*made)
     return (
         res.reshape(64, 4, 1, 1024),
         gf.reshape(4, 512, 1, 128),
-        k[4:8, :31],
-        k[0:4, :31],
-        w[64:128],
-        w[0:64].T,
+        grad_kz,
+        grad_kx,
+        grad_in,
+        grad_out.T,
     )
 
 

time: 65.9 us -> 58.6 us (0.89)
  local copies, waits for them, and re-layouts: 7.51 us -> 0 us
  Pallas kernels: 56.9 us -> 57.8 us
    reshape x2 -> x0, local copies, waits for them, and re-layouts: 4.05 us -> none  [the longest x1 2.09 us: local(): res.reshape(64, 4, 1, 1024)]
    pallas_call x0 -> x1, Pallas kernels: none -> 2.23 us  [local(): pl.pallas_call(write_kernel, out_shape=tuple((jax.ShapeDtypeStruct(m.shap...]
    unnamed x11 -> x0, local copies, waits for them, and re-layouts: 2.06 us -> none
    pallas_call x1, Pallas kernels: 56.9 us -> 55.6 us  [local(): pl.pallas_call(functools.partial(kernel, npx, npc, scale), out_shape=(jax...]
where the time goes in v2:
time: 58.6 us; the launch traced here: 58.5 us
  Pallas kernels  57.8 us (99%)
  between operations  0.64 us (1%)
    pallas_call x1, Pallas kernels, local(): pl.pallas_call(functools.partial(kernel, npx, npc, scale), out_shape=(jax...  55.6 us
    pallas_call x1, Pallas kernels, local(): pl.pallas_call(write_kernel, out_shape=tuple((jax.ShapeDtypeStruct(m.shap...  2.23 us

profile of v2, /device:TPU:1, one launch (start us, length us, event | category | flops | bytes accessed | tf_op | source)
XLA Modules:
  0.0 58.5 jit_solution(15862126795630706061)
XLA Ops:
  0.6 55.6 %shard_map.109 = (bf16[64,4,1024]{2,1,0:T(4,128)(2,1)}, bf16[4,512,128]{2,1,0:T(8,128)(2,1)}, f32[4,31]{1,0:T(4,128)}, f32[4,31]{1,0:T(4,128)}, f32[64,128]{1,0:T(8,128)}, /*index=5*/f32[64,128]{1,0:T(8,128)}) custom-call(bf16[4,512,128]{2,1,0:T(8,128)(2,1)} %bitcast.10, bf16[64,4,1024]{2,1,0:T(4,128)(2,1)} %bitcast.11, bf16[4,31]{1,0:T(4,128)(2,1)} %kz.1, ...), custom_call_target="tpu_custom_call" | custom-call | tf_op jit(solution)/shard_map/pallas_call | solution.py:365
  56.2 2.2 %shard_map.110 = (bf16[64,4,1024]{2,1,0:T(4,128)(2,1)}, bf16[4,512,128]{2,1,0:T(8,128)(2,1)}, f32[4,31]{1,0:T(4,128)}, f32[4,31]{1,0:T(4,128)}, f32[64,128]{1,0:T(8,128)}, /*index=5*/f32[64,128]{1,0:T(8,128)}) custom-call(bf16[64,4,1024]{2,1,0:T(4,128)(2,1)} %get-tuple-element.18.refs_0_, bf16[4,512,128]{2,1,0:T(8,128)(2,1)} %get-tuple-element.19.refs_1_, ...), custom_call_target="tpu_custom_call" | custom-call | tf_op jit(solution)/shard_map/pallas_call | solution.py:424

commit v3 on v2

--- a/solution.py
+++ b/solution.py
@@ -88,14 +88,24 @@
 
 def kernel(
     npx, npc, scale,
-    field, cot, kz, kx, w_in, w_ot,
+    field_h, cot_h, kz_h, kx_h, w_in_h, w_ot_h,
     res_out, gf_out, kz_out, kx_out, wi_out, wo_out,
+    field, cot, kz, kx, w_in, w_ot, in_sem,
     taps, fs, kfe, bands, az, aze, hs, hr, xe, mx, ss, sr, mixd, cotp, resp, bkp, bs, br, gbx, hs2, hr2,
     wacc, rs1, rs2, rs2s, wfin, kp, kr,
     send, recv, all_send, all_recv, halo_send, halo_recv,
 ):
     px = lax.axis_index("px")
     pc = lax.axis_index("pc")
+
+    loads = [
+        pltpu.make_async_copy(source, target, in_sem.at[k])
+        for k, (source, target) in enumerate(
+            ((kz_h, kz), (kx_h, kx), (field_h, field), (w_in_h, w_in), (w_ot_h, w_ot), (cot_h, cot))
+        )
+    ]
+    for load in loads:
+        load.start()
 
     barrier = pltpu.get_barrier_semaphore()
 
@@ -177,6 +187,8 @@
         before = (into[1].astype(F32) * keep_before).astype(BF)
         return mm_nt(jnp.concatenate([after, before], axis=1), pick).astype(BF)
 
+    loads[0].wait()
+    loads[1].wait()
     taps[...] = jnp.zeros_like(taps)
     taps[0:4, 0:31] = kz[...].astype(F32)
     taps[8:12, 0:31] = kx[...].astype(F32)
@@ -189,6 +201,7 @@
     pick = ones_where(
         (row // 128 == (col % 128) // 16) & (row % 128 == col % 16 + jnp.where(col < 128, 0, 112))
     )
+    loads[2].wait()
     for c in range(4):
         for i in range(8):
             fs[64 * c : 64 * c + 64, 128 * i : 128 * i + 128] = field[c, 64 * i : 64 * i + 64, :]
@@ -211,6 +224,8 @@
     halo = halo_start(0, packed, hs, hr)
     along_z(fs, az)
 
+    for load in loads[3:]:
+        load.wait()
     shape = (256, 256)
     row, col = iota(shape, 0), iota(shape, 1)
     to_dest = ones_where(col == ((row // 4) % 4) * 64 + (row // 16) * 4 + row % 4)
@@ -285,7 +300,7 @@
             wacc[64:128, :] += mm_nt(low, grad_hid)
             return carry
 
-        lax.fori_loop(0, 4, cells, 0)
+        lax.fori_loop(0, 4, cells, 0, unroll=4)
         made = mm(from_cells, bkp[...]).astype(BF)
         bs[i0] = made[:, :128].reshape(npc, 16, 128)
         bs[i1] = made[:, 128:].reshape(npc, 16, 128)
@@ -372,9 +387,16 @@
             jax.ShapeDtypeStruct((64, 128), F32),
             jax.ShapeDtypeStruct((64, 128), F32),
         ),
-        in_specs=[vmem] * 6,
+        in_specs=[pl.BlockSpec(memory_space=pltpu.HBM)] * 6,
         out_specs=(vmem,) * 6,
         scratch_shapes=[
+            pltpu.VMEM((4, 512, 128), BF),
+            pltpu.VMEM((64, 4, 1024), BF),
+            pltpu.VMEM((4, 31), BF),
+            pltpu.VMEM((4, 31), BF),
+            pltpu.VMEM((64, 128), BF),
+            pltpu.VMEM((64, 128), BF),
+            pltpu.SemaphoreType.DMA((6,)),
             pltpu.VMEM((16, 256), F32),
             pltpu.VMEM((256, 1024), BF),
             pltpu.VMEM((4, 256, 512), BF),

time: 58.6 us -> 56.7 us (0.968)
  Pallas kernels: 57.8 us -> 55.9 us
    pallas_call x1, Pallas kernels: 55.6 us -> 53.7 us  [local(): pl.pallas_call(functools.partial(kernel, npx, npc, scale), out_shape=(jax...]
where the time goes in v3:
time: 56.7 us; the launch traced here: 56.5 us
  Pallas kernels  55.9 us (99%)
  between operations  0.64 us (1%)
    pallas_call x1, Pallas kernels, local(): pl.pallas_call(functools.partial(kernel, npx, npc, scale), out_shape=(jax...  53.7 us
    pallas_call x1, Pallas kernels, local(): pl.pallas_call(write_kernel, out_shape=tuple((jax.ShapeDtypeStruct(m.shap...  2.23 us

profile of v3, /device:TPU:1, one launch (start us, length us, event | category | flops | bytes accessed | tf_op | source)
XLA Modules:
  0.0 56.5 jit_solution(15046395356896792213)
XLA Ops:
  0.6 53.7 %shard_map.109 = (bf16[64,4,1024]{2,1,0:T(4,128)(2,1)}, bf16[4,512,128]{2,1,0:T(8,128)(2,1)}, f32[4,31]{1,0:T(4,128)}, f32[4,31]{1,0:T(4,128)}, f32[64,128]{1,0:T(8,128)}, /*index=5*/f32[64,128]{1,0:T(8,128)}) custom-call(bf16[4,512,128]{2,1,0:T(8,128)(2,1)} %bitcast.10, bf16[64,4,1024]{2,1,0:T(4,128)(2,1)} %bitcast.11, bf16[4,31]{1,0:T(4,128)(2,1)} %kz_h.1, ...), custom_call_target="tpu_custom_call" | custom-call | tf_op jit(solution)/shard_map/pallas_call | solution.py:380
  54.3 2.2 %shard_map.110 = (bf16[64,4,1024]{2,1,0:T(4,128)(2,1)}, bf16[4,512,128]{2,1,0:T(8,128)(2,1)}, f32[4,31]{1,0:T(4,128)}, f32[4,31]{1,0:T(4,128)}, f32[64,128]{1,0:T(8,128)}, /*index=5*/f32[64,128]{1,0:T(8,128)}) custom-call(bf16[64,4,1024]{2,1,0:T(4,128)(2,1)} %get-tuple-element.18.refs_0_, bf16[4,512,128]{2,1,0:T(8,128)(2,1)} %get-tuple-element.19.refs_1_, ...), custom_call_target="tpu_custom_call" | custom-call | tf_op jit(solution)/shard_map/pallas_call | solution.py:446
